TPU v7x, 32 devices: a whole 2x2x4 slice. The times are simulated.
32 devices in a mesh: groups: 2 (over x), weight: 16 (over z, y, core).
Axes of the slice: x: 2, y: 2, z: 4, core: 2. Of those that a mesh axis runs over, the one named last changes fastest.
Arguments:
- hidden: bfloat16 [128, 8192], P(('groups', 'weight')), parts along dimension 0, may hold values from -6 to 6
- norm_gain: float32 [8192], replicated, may hold values from 0.1 to 1.9
- in_weight: bfloat16 [8192, 2, 8192], P(None, None, 'weight'), may hold values from -0.0625 to 0.0625
- conv_weight: float32 [4, 8192], P(None, 'weight'), may hold values from -0.6 to 0.6
- conv_offset: float32 [8192], P('weight'), may hold values from -0.5 to 0.5
- coef_weight: bfloat16 [8192, 544], P('weight'), may hold values from -0.0625 to 0.0625
- step_weight: bfloat16 [512, 8192], P(None, 'weight'), may hold values from -0.25 to 0.25
- step_bias: float32 [8192], P('weight'), may hold values from -3 to 0.5
- log_rates: float32 [16, 8192], P(None, 'weight'), may hold values from 0 to 2.77
- skip_gain: float32 [8192], P('weight'), may hold values from 0.5 to 1.5
- out_weight: bfloat16 [8192, 8192], P('weight'), may hold values from -0.0625 to 0.0625
- ssm_state: bfloat16 [128, 16, 8192], P('groups', None, 'weight'), parts along dimension 0, may hold values from -6 to 6
- conv_state: bfloat16 [128, 3, 8192], P('groups', None, 'weight'), parts along dimension 0, may hold values from -6 to 6
- live_counts: int32 [32], P('groups'), parts along dimension 0, may hold values from 1 to 3, as said below
Outputs:
- mixed: bfloat16 [128, 8192], P(('groups', 'weight')), parts along dimension 0
- new_state: bfloat16 [128, 16, 8192], P('groups', None, 'weight'), parts along dimension 0
- new_conv: bfloat16 [128, 3, 8192], P('groups', None, 'weight'), parts along dimension 0
There are 2 independent parts, one for each index of `groups`. A program takes and returns all parts, laid end to end along the dimension named above; an argument that names none is the same for every part. Nothing has to cross between parts.
Inputs may be any that keep to these rules, and one draw needn't show every extreme that they name: The live rows of a microbatch are its first live_counts rows; the most, 3, is reached by some microbatch.
All inputs are finite; a program needn't handle non-finite values.
Results may differ from a plain program's by a relative error of at most 0.0039.
Values may be sent and summed in bfloat16 or wider, within the bound.
A program may use at most 64 MiB of HBM per device.

v0:
```python
import jax
import jax.numpy as jnp
from jax import lax
from jax.sharding import PartitionSpec as P

NSTATE = 16
DTR = 512
LIVE_MAX = 3


def rms_normed(hidden, norm_gain):
    wide = hidden.astype(jnp.float32)
    factor = lax.rsqrt(jnp.mean(wide * wide, axis=-1, keepdims=True) + 1e-05)
    return (wide * factor * norm_gain).astype(jnp.bfloat16)


def body(
    hidden,
    norm_gain,
    in_weight,
    conv_weight,
    conv_offset,
    coef_weight,
    step_weight,
    step_bias,
    log_rates,
    skip_gain,
    out_weight,
    ssm_state,
    conv_state,
    live_counts,
):
    devices = lax.axis_size("weight")
    rows_dev = hidden.shape[0]
    channels = in_weight.shape[2]
    states_n = ssm_state.shape[1]
    kept = LIVE_MAX
    normed = rms_normed(hidden[:kept], norm_gain)
    joined = in_weight.reshape(in_weight.shape[0], 2 * channels)
    both = jnp.dot(
        lax.all_gather(normed, "weight", axis=0, tiled=True),
        joined,
        preferred_element_type=jnp.float32,
    )
    total_rows = both.shape[0]
    conv_input = both[:, :channels].astype(jnp.bfloat16)
    gate_branch = both[:, channels:]
    state_grid = ssm_state.reshape(devices, rows_dev, states_n, channels)
    conv_grid = conv_state.reshape(devices, rows_dev, 3, channels)
    state_kept = state_grid[:, :kept].reshape(total_rows, states_n, channels)
    conv_kept = conv_grid[:, :kept].reshape(total_rows, 3, channels)
    row_ids = jnp.arange(total_rows, dtype=jnp.int32)
    per_row = jnp.repeat(live_counts, kept, total_repeat_length=total_rows)
    alive = row_ids % kept < per_row
    window = jnp.concatenate([conv_kept, conv_input[:, None, :]], axis=1)
    convolved = jnp.sum(window.astype(jnp.float32) * conv_weight[None], axis=1) + conv_offset
    mixed_x = jax.nn.silu(convolved).astype(jnp.bfloat16)
    partial_low = jnp.dot(mixed_x, coef_weight, preferred_element_type=jnp.float32)
    low_rank = lax.psum(partial_low, "weight")
    step_low = low_rank[:, :DTR].astype(jnp.bfloat16)
    in_coef = low_rank[:, DTR : DTR + NSTATE]
    out_coef = low_rank[:, DTR + NSTATE :]
    step_size = jax.nn.softplus(
        jnp.dot(step_low, step_weight, preferred_element_type=jnp.float32) + step_bias
    )
    x_wide = mixed_x.astype(jnp.float32)
    decays = jnp.exp(-step_size[:, None, :] * jnp.exp(log_rates)[None])
    old_state = state_kept.astype(jnp.float32)
    updated = decays * old_state + step_size[:, None, :] * in_coef[:, :, None] * x_wide[:, None, :]
    readout = jnp.sum(out_coef[:, :, None] * updated, axis=1) + skip_gain * x_wide
    gated_out = jnp.where(alive[:, None], readout * jax.nn.silu(gate_branch), 0.0).astype(
        jnp.bfloat16
    )
    block = lax.slice_in_dim(gated_out, 0, lax.axis_size("weight") * kept, axis=0)
    mixer_term = lax.psum_scatter(
        jnp.dot(block, out_weight, preferred_element_type=jnp.float32),
        "weight",
        scatter_dimension=0,
        tiled=True,
    )
    own_mixed = (hidden[:kept].astype(jnp.float32) + mixer_term).astype(jnp.bfloat16)
    mixed = jnp.concatenate([own_mixed, hidden[kept:]], axis=0)
    state_new_kept = jnp.where(alive[:, None, None], updated, old_state).astype(jnp.bfloat16)
    conv_new_kept = jnp.where(alive[:, None, None], window[:, 1:], conv_kept)
    new_state = jnp.concatenate(
        [state_new_kept.reshape(devices, kept, states_n, channels), state_grid[:, kept:]], axis=1
    ).reshape(ssm_state.shape)
    new_conv = jnp.concatenate(
        [conv_new_kept.reshape(devices, kept, 3, channels), conv_grid[:, kept:]], axis=1
    ).reshape(conv_state.shape)
    return (mixed, new_state, new_conv)


def solution(mesh):
    in_specs = (
        P(("groups", "weight"), None),
        P(),
        P(None, None, "weight"),
        P(None, "weight"),
        P("weight"),
        P("weight", None),
        P(None, "weight"),
        P("weight"),
        P(None, "weight"),
        P("weight"),
        P("weight", None),
        P("groups", None, "weight"),
        P("groups", None, "weight"),
        P("groups"),
    )
    out_specs = (
        P(("groups", "weight"), None),
        P("groups", None, "weight"),
        P("groups", None, "weight"),
    )
    return jax.shard_map(body, mesh=mesh, in_specs=in_specs, out_specs=out_specs, check_vma=False)
```

profile of v0, /device:TPU:0, one launch (start us, length us, event | category | flops | bytes accessed | tf_op | source)
XLA Modules:
  0.0 255.2 jit_solution(7793074444627123706)
XLA Ops:
  7.2 0.0 copy-start
  7.2 0.0 all-reduce.4.cloned.1.call-start
  7.2 1.1 fusion.4
  8.3 1.0 fusion.8
  9.3 26.3 %all-gather = bf16[16,3,8192]{2,1,0:T(4,128)(2,1)S(1)} all-gather(bf16[1,3,8192]{2,1,0:T(4,128)(2,1)S(1)} %fusion.8), channel_id=1, replica_groups=mesh['groups'=2,'weight'=16] {'weight'}, dimensions={0}, use_global_device_ids=true | all-gather | bytes 835584 | tf_op jit(solution)/shard_map/all_gather | solution.py:41
  35.5 0.7 reshape.164
  36.2 11.4 %copy.19 = bf16[1024,8,2,512]{3,1,2,0:T(8,128)(2,1)S(1)} copy(bf16[1024,8,2,512]{3,2,1,0:T(2,128)(2,1)} %bitcast.24) | data formatting | bytes 33554432
  47.6 0.0 copy-start.7
  47.6 0.0 copy-start.10
  47.7 0.0 copy-start.8
  47.7 3.1 %fusion.26 = f32[48,1024]{1,0:T(8,128)S(1)} fusion(bf16[48,8192]{1,0:T(8,128)(2,1)S(1)} %reshape.164, bf16[8192,1024]{1,0:T(8,128)(2,1)S(1)} %bitcast.23), kind=kOutput, calls=%fused_computation.53 | convolution fusion | flops 805306368 | bytes 17760256 | tf_op jit(solution)/shard_map/dot_general | solution.py:40
  50.8 0.0 copy-start.13
  50.8 0.0 copy-start.1
  50.8 0.0 copy-done.7
  50.8 0.0 copy-start.5
  50.8 0.0 copy-start.9
  50.8 0.1 reshape.148
  50.9 0.0 copy-start.4
  50.9 0.0 copy-start.12
  50.9 0.1 reshape.149
  51.0 0.0 copy-done.10
  51.1 0.0 copy-done
  51.1 0.0 copy-done.8
  51.1 0.9 fusion.23
  52.1 0.0 copy-start.2
  52.1 0.0 all-reduce.4.cloned.1.call-update
  52.1 0.0 all-reduce.6.cloned.1.call-start
  52.2 0.1 fusion.14
  52.2 0.0 copy-done.13
  52.3 0.0 copy-done.1
  52.3 0.8 gather_fusion
  53.1 0.1 gather.7
  53.1 0.6 fusion.16
  53.8 0.6 fusion.20
  54.3 0.1 copy.18
  54.4 0.0 copy-done.5
  54.4 0.0 copy-done.9
  54.4 0.6 exp.27
  55.1 81.9 %all-reduce.4.cloned.1.call-done = f32[48,544]{1,0:T(8,128)} async-done(((f32[48,544]{1,0:T(8,128)}), f32[48,544]{1,0:T(8,128)}) %all-reduce.4.cloned.1.call-update) | async-done | bytes 104464 | tf_op jit(solution)/shard_map/psum | solution.py:59
  137.0 0.9 fusion.24
  137.9 0.6 mul.130
  138.5 0.0 copy-done.4
  138.5 0.0 copy-done.12
  138.5 1.1 fusion.25
  139.8 0.6 mul.121
  140.4 0.0 copy-done.2
  140.4 1.7 fusion.1
  142.1 0.1 reduce_sum.35
  142.2 6.2 %fusion.9 = f32[48,8192]{1,0:T(8,128)} fusion(bf16[512,8192]{1,0:T(8,128)(2,1)} %param.26, f32[48,1024]{1,0:T(8,128)S(1)} %fusion.26, f32[48,512]{1,0:T(8,128)S(1)} %reduce_sum.35, f32[512]{0:T(512)} %param.25, pred[48]{0:T(512)(128)(4,1)} %fusion.20, f32[48,512]{1,0:T(8,128)S(1)} %multiply_reduce_fusion.1, f32[512]{0:T(512)} %param.20), kind=kOutput, calls=%fused_computation.31 | convolution fusion | flops 403046400 | bytes 10260528 | tf_op jit(solution)/shard_map/dot_general | solution.py:76
  148.4 0.0 all-reduce.6.cloned.1.call-update
  148.4 0.8 copy-done.3
  149.3 0.1 slice.76
  149.4 0.0 copy-done.6
  149.4 0.0 copy-done.11
  149.4 0.1 fusion.3
  149.5 0.1 reshape.153
  149.6 0.2 pad_maximum_fusion.2
  149.8 0.7 reshape.154
  150.5 0.0 copy-done.14
  150.6 0.6 dynamic-slice.6
  151.8 1.1 pad_maximum_fusion
  152.9 93.7 %all-reduce.6.cloned.1.call-done = f32[48,8192]{1,0:T(8,128)} async-done(((f32[48,8192]{1,0:T(8,128)}), f32[48,8192]{1,0:T(8,128)}) %all-reduce.6.cloned.1.call-update) | async-done | bytes 1572880
  246.6 1.1 fusion.7
  247.7 0.7 pad_maximum_fusion.3
  (13 shorter events, 0.3 us)
Async XLA Ops:
  7.2 43.9 %copy-start = (bf16[512,544]{0,1:T(8,128)(2,1)S(1)}, bf16[512,544]{0,1:T(8,128)(2,1)}, u32[]{:S(2)}) copy-start(bf16[512,544]{0,1:T(8,128)(2,1)} %param.21) | copy-start | bytes 1671172
  7.2 129.8 %all-reduce.4.cloned.1.call-start = ((), (), s32[]{:S(2)}) async-start(), calls=%async_computation | async-start | bytes 245760 | tf_op jit(solution)/shard_map/psum | solution.py:59
  47.6 3.2 %copy-start.7 = (bf16[64,3,512]{2,0,1:T(8,128)(2,1)S(1)}, bf16[64,3,512]{2,0,1:T(8,128)(2,1)}, u32[]{:S(2)}) copy-start(bf16[64,3,512]{2,0,1:T(8,128)(2,1)} %param.28) | copy-start | bytes 589828
  47.6 3.4 %copy-start.10 = (f32[4,512]{1,0:T(4,128)S(1)}, f32[4,512]{1,0:T(4,128)}, u32[]{:S(2)}) copy-start(f32[4,512]{1,0:T(4,128)} %param.19) | copy-start | bytes 24580
  47.7 3.5 %copy-start.8 = (f32[512]{0:T(512)S(1)}, f32[512]{0:T(512)}, u32[]{:S(2)}) copy-start(f32[512]{0:T(512)} %param.20) | copy-start | bytes 6148
  50.8 1.5 copy-start.13
  50.8 1.5 copy-start.1
  50.8 3.6 %copy-start.5 = (bf16[48,1,512]{2,0,1:T(8,128)(2,1)}, bf16[48,1,512]{2,0,1:T(8,128)(2,1)S(1)}, u32[]{:S(2)}) copy-start(bf16[48,1,512]{2,0,1:T(8,128)(2,1)S(1)} %fusion.10) | copy-start | bytes 147460
  50.8 3.6 %copy-start.9 = (f32[16,512]{1,0:T(8,128)S(1)}, f32[16,512]{1,0:T(8,128)}, u32[]{:S(2)}) copy-start(f32[16,512]{1,0:T(8,128)} %param.24) | copy-start | bytes 98308
  50.9 87.6 %copy-start.4 = (bf16[512,512]{1,0:T(8,128)(2,1)S(1)}, bf16[512,512]{1,0:T(8,128)(2,1)}, u32[]{:S(2)}) copy-start(bf16[512,512]{1,0:T(8,128)(2,1)} %param.22) | copy-start | bytes 1572868
  50.9 87.6 %copy-start.12 = (f32[512]{0:T(512)S(1)}, f32[512]{0:T(512)}, u32[]{:S(2)}) copy-start(f32[512]{0:T(512)} %param.23) | copy-start | bytes 6148
  52.1 88.3 %copy-start.2 = (bf16[64,16,512]{2,1,0:T(8,128)(2,1)S(1)}, bf16[64,16,512]{2,1,0:T(8,128)(2,1)}, u32[]{:S(2)}) copy-start(bf16[64,16,512]{2,1,0:T(8,128)(2,1)} %param.27) | copy-start | bytes 3145732
  52.1 194.5 %all-reduce.6.cloned.1.call-start = ((), (), s32[]{:S(2)}) async-start(), calls=%async_computation.1 | async-start | bytes 3145728
  148.4 0.8 copy-start.3
  148.4 1.0 copy-start.6
  148.4 1.0 copy-start.11
  149.2 1.3 copy-start.14
Sparse Core Ops, SparseCore 0:
  52.2 84.7 all-reduce.3
  148.5 98.0 all-reduce.5
where the time goes:
time: 256 us; the launch traced here: 255 us
  waiting for transfers between devices  176 us (69%)
  blocking collectives  26.3 us (10%)
  local copies, waits for them, and re-layouts  18.6 us (7%)
  between operations  15 us (6%)
  matrix products  11.3 us (4%)
  other arithmetic  8.21 us (3%)
    unnamed x3, waiting for transfers between devices  93.8 us
    psum x1, waiting for transfers between devices, body(): low_rank = lax.psum(partial_low, 'weight')  81.9 us
    all_gather x1, blocking collectives, body(): lax.all_gather(normed, 'weight', axis=0, tiled=True)  26.3 us
    unnamed x33, local copies, waits for them, and re-layouts  13.6 us
    dot_general x1, matrix products, body(): jnp.dot(block, out_weight, preferred_element_type=jnp.float32)  6.19 us
  transfers between devices with their start and end apart: 2, of which 2 were waited for; matrix products, arithmetic and copies ran while one was open for 2% of the time, Pallas kernels for 0%

commit v1 on v0

--- a/solution.py
+++ b/solution.py
@@ -56,7 +56,7 @@
     convolved = jnp.sum(window.astype(jnp.float32) * conv_weight[None], axis=1) + conv_offset
     mixed_x = jax.nn.silu(convolved).astype(jnp.bfloat16)
     partial_low = jnp.dot(mixed_x, coef_weight, preferred_element_type=jnp.float32)
-    low_rank = lax.psum(partial_low, "weight")
+    low_rank = jnp.sum(lax.all_gather(partial_low, "weight"), axis=0)
     step_low = low_rank[:, :DTR].astype(jnp.bfloat16)
     in_coef = low_rank[:, DTR : DTR + NSTATE]
     out_coef = low_rank[:, DTR + NSTATE :]

time: 256 us -> 206 us (0.80)
  waiting for transfers between devices: 176 us -> 126 us
    psum x1 -> x0, waiting for transfers between devices: 81.9 us -> none  [body(): low_rank = lax.psum(partial_low, 'weight')]
    all_gather x0 -> x1, waiting for transfers between devices: none -> 35.4 us  [body(): low_rank = jnp.sum(lax.all_gather(partial_low, 'weight'), axis=0)]
    unnamed x3, waiting for transfers between devices: 93.8 us -> 90.2 us
  transfers between devices with their start and end apart: 2 -> 2, of which waited for: 2 -> 2; matrix products, arithmetic and copies ran while one was open for 2% -> 3% of each run, Pallas kernels for 0% -> 0%
where the time goes in v1:
time: 206 us; the launch traced here: 205 us
  waiting for transfers between devices  126 us (61%)
  blocking collectives  26.3 us (13%)
  local copies, waits for them, and re-layouts  17.8 us (9%)
  between operations  15 us (7%)
  matrix products  10.5 us (5%)
  other arithmetic  9.95 us (5%)
    unnamed x3, waiting for transfers between devices  90.2 us
    all_gather x1, waiting for transfers between devices, body(): low_rank = jnp.sum(lax.all_gather(partial_low, 'weight'), axis=0)  35.4 us
    all_gather x1, blocking collectives, body(): lax.all_gather(normed, 'weight', axis=0, tiled=True)  26.3 us
    unnamed x33, local copies, waits for them, and re-layouts  13.6 us
    dot_general x1, matrix products, body(): jnp.dot(block, out_weight, preferred_element_type=jnp.float32)  6.19 us
  transfers between devices with their start and end apart: 2, of which 2 were waited for; matrix products, arithmetic and copies ran while one was open for 3% of the time, Pallas kernels for 0%

profile of v1, /device:TPU:0, one launch (start us, length us, event | category | flops | bytes accessed | tf_op | source)
XLA Modules:
  0.0 205.2 jit_solution(17757245868268286427)
XLA Ops:
  7.2 0.0 copy-start
  7.2 0.0 all-gather.4.cloned.1.call-start
  7.2 1.1 fusion.4
  8.3 1.0 fusion.8
  9.3 26.3 %all-gather.1 = bf16[16,3,8192]{2,1,0:T(4,128)(2,1)S(1)} all-gather(bf16[1,3,8192]{2,1,0:T(4,128)(2,1)S(1)} %fusion.8), channel_id=1, replica_groups=mesh['groups'=2,'weight'=16] {'weight'}, dimensions={0}, use_global_device_ids=true | all-gather | bytes 835584 | tf_op jit(solution)/shard_map/all_gather | solution.py:41
  35.5 0.7 reshape.165
  36.2 11.4 %copy.19 = bf16[1024,8,2,512]{3,1,2,0:T(8,128)(2,1)S(1)} copy(bf16[1024,8,2,512]{3,2,1,0:T(2,128)(2,1)} %bitcast.25) | data formatting | bytes 33554432
  47.6 0.0 copy-start.7
  47.6 0.0 copy-start.10
  47.7 0.0 copy-start.8
  47.7 3.1 %fusion.26 = f32[48,1024]{1,0:T(8,128)S(1)} fusion(bf16[48,8192]{1,0:T(8,128)(2,1)S(1)} %reshape.165, bf16[8192,1024]{1,0:T(8,128)(2,1)S(1)} %bitcast.24), kind=kOutput, calls=%fused_computation.53 | convolution fusion | flops 805306368 | bytes 17760256 | tf_op jit(solution)/shard_map/dot_general | solution.py:40
  50.8 0.0 copy-start.9
  50.8 0.0 copy-start.13
  50.8 0.0 copy-start.1
  50.8 0.0 copy-done.7
  50.8 0.0 copy-start.5
  50.8 0.1 reshape.148
  50.9 0.1 reshape.149
  51.0 0.0 copy-done.10
  51.1 0.0 copy-done
  51.1 0.0 copy-done.8
  51.1 0.9 fusion.23
  52.0 0.0 all-gather.4.cloned.1.call-update
  52.1 0.0 copy-done.5
  52.1 0.0 all-reduce.3.cloned.1.call-start
  52.2 0.1 fusion.14
  52.2 0.0 copy-start.4
  52.2 0.0 copy-start.12
  52.3 0.1 copy.18
  52.3 0.0 copy-done.9
  52.3 0.6 exp.27
  53.0 0.0 copy-done.13
  53.0 0.0 copy-done.1
  53.0 0.8 gather_fusion
  53.8 0.1 gather.7
  53.8 0.6 fusion.20
  54.4 0.6 fusion.16
  55.0 35.4 %all-gather.4.cloned.1.call-done = f32[768,544]{1,0:T(8,128)} async-done(((f32[48,544]{1,0:T(8,128)}), f32[768,544]{1,0:T(8,128)}) %all-gather.4.cloned.1.call-update) | async-done | bytes 1671184 | tf_op jit(solution)/shard_map/all_gather | solution.py:59
  90.5 1.7 reduce_sum.42
  92.2 0.1 fusion.24
  92.3 0.6 mul.130
  92.9 0.0 copy-done.4
  92.9 0.0 copy-done.12
  93.0 0.3 fusion.25
  93.3 0.6 mul.121
  93.9 0.0 copy-done.2
  93.9 1.7 fusion.1
  95.7 0.1 reduce_sum.45
  95.7 6.2 %fusion.9 = f32[48,8192]{1,0:T(8,128)} fusion(bf16[512,8192]{1,0:T(8,128)(2,1)} %param.26, f32[48,1024]{1,0:T(8,128)S(1)} %fusion.26, f32[48,512]{1,0:T(8,128)S(1)} %reduce_sum.45, f32[512]{0:T(512)} %param.25, pred[48]{0:T(512)(128)(4,1)} %fusion.20, f32[48,512]{1,0:T(8,128)S(1)} %multiply_reduce_fusion.1, f32[512]{0:T(512)} %param.20), kind=kOutput, calls=%fused_computation.31 | convolution fusion | flops 403046400 | bytes 10260528 | tf_op jit(solution)/shard_map/dot_general | solution.py:76
  101.9 0.0 all-reduce.3.cloned.1.call-update
  101.9 0.8 copy-done.3
  102.8 0.1 slice.76
  102.9 0.0 copy-done.6
  103.0 0.0 copy-done.11
  103.0 0.1 fusion.3
  103.0 0.1 reshape.153
  103.1 0.2 pad_maximum_fusion.2
  103.4 0.7 reshape.154
  104.1 0.0 copy-done.14
  104.1 0.6 dynamic-slice.6
  105.3 1.1 pad_maximum_fusion
  106.4 90.2 %all-reduce.3.cloned.1.call-done = f32[48,8192]{1,0:T(8,128)} async-done(((f32[48,8192]{1,0:T(8,128)}), f32[48,8192]{1,0:T(8,128)}) %all-reduce.3.cloned.1.call-update) | async-done | bytes 1572880
  196.6 1.1 fusion.7
  197.7 0.7 pad_maximum_fusion.3
  (14 shorter events, 0.3 us)
Async XLA Ops:
  7.2 43.9 %copy-start = (bf16[512,544]{0,1:T(8,128)(2,1)S(1)}, bf16[512,544]{0,1:T(8,128)(2,1)}, u32[]{:S(2)}) copy-start(bf16[512,544]{0,1:T(8,128)(2,1)} %param.21) | copy-start | bytes 1671172
  7.2 83.3 %all-gather.4.cloned.1.call-start = ((), (), s32[]{:S(2)}) async-start(), calls=%async_computation | async-start | bytes 2088960 | tf_op jit(solution)/shard_map/all_gather | solution.py:59
  47.6 3.2 %copy-start.7 = (bf16[64,3,512]{2,0,1:T(8,128)(2,1)S(1)}, bf16[64,3,512]{2,0,1:T(8,128)(2,1)}, u32[]{:S(2)}) copy-start(bf16[64,3,512]{2,0,1:T(8,128)(2,1)} %param.28) | copy-start | bytes 589828
  47.6 3.4 %copy-start.10 = (f32[4,512]{1,0:T(4,128)S(1)}, f32[4,512]{1,0:T(4,128)}, u32[]{:S(2)}) copy-start(f32[4,512]{1,0:T(4,128)} %param.19) | copy-start | bytes 24580
  47.7 3.4 %copy-start.8 = (f32[512]{0:T(512)S(1)}, f32[512]{0:T(512)}, u32[]{:S(2)}) copy-start(f32[512]{0:T(512)} %param.20) | copy-start | bytes 6148
  50.8 1.6 copy-start.9
  50.8 2.2 %copy-start.13 = (s32[48]{0:T(128)S(1)}, s32[48]{0:T(128)}, u32[]{:S(2)}) copy-start(s32[48]{0:T(128)} %constant.113) | copy-start | bytes 580
  50.8 2.2 %copy-start.1 = (s32[16]{0:T(128)S(1)}, s32[16]{0:T(128)}, u32[]{:S(2)}) copy-start(s32[16]{0:T(128)} %param.29) | copy-start | bytes 196
  50.8 1.2 copy-start.5
  52.1 144.5 %all-reduce.3.cloned.1.call-start = ((), (), s32[]{:S(2)}) async-start(), calls=%async_computation.1 | async-start | bytes 3145728
  52.2 40.7 %copy-start.4 = (bf16[512,512]{1,0:T(8,128)(2,1)S(1)}, bf16[512,512]{1,0:T(8,128)(2,1)}, u32[]{:S(2)}) copy-start(bf16[512,512]{1,0:T(8,128)(2,1)} %param.22) | copy-start | bytes 1572868
  52.2 40.7 %copy-start.12 = (f32[512]{0:T(512)S(1)}, f32[512]{0:T(512)}, u32[]{:S(2)}) copy-start(f32[512]{0:T(512)} %param.23) | copy-start | bytes 6148
  90.5 3.4 %copy-start.2 = (bf16[64,16,512]{2,1,0:T(8,128)(2,1)S(1)}, bf16[64,16,512]{2,1,0:T(8,128)(2,1)}, u32[]{:S(2)}) copy-start(bf16[64,16,512]{2,1,0:T(8,128)(2,1)} %param.27) | copy-start | bytes 3145732
  101.9 0.8 copy-start.3
  101.9 1.0 copy-start.6
  101.9 1.0 copy-start.11
  102.7 1.3 copy-start.14
Sparse Core Ops, SparseCore 0:
  52.2 38.2 all-gather.3
  102.1 94.4 all-reduce.2
